TPU v7x, 512 devices: a whole 4x4x16 slice. The times are simulated.
512 devices in a mesh: leaf: 128 (over z, y, core), rep: 4 (over x).
Axes of the slice: x: 4, y: 4, z: 16, core: 2. Of those that a mesh axis runs over, the one named last changes fastest.
Arguments:
- positions: float32 [3, 8192, 128], P(None, ('leaf', 'rep')), may hold values from -6 to 6
- density: float32 [3, 8192, 128], P(None, ('leaf', 'rep')), may hold values from -6 to 6
- near_offset: int32 [8192, 12], P(('leaf', 'rep')), may hold values from -2 to 2
- near_count: int32 [8192], P(('leaf', 'rep')), may hold values from 1 to 12
- inter_list: int32 [512, 189], P(('leaf', 'rep')), may hold values from 0 to 511
- operator_index: int32 [512, 189], P(('leaf', 'rep')), may hold values from 0 to 3
- lattice_index: int32 [512], P(('leaf', 'rep')), may hold values from 0 to 1
- up_weight: bfloat16 [512, 384], replicated, may hold values from -0.3125 to 0.3125
- m2l_operators: bfloat16 [4, 512, 512], replicated, may hold values from -0.0390625 to 0.0390625
- lattice_operators: bfloat16 [2, 512, 512], replicated, may hold values from -0.01171875 to 0.01171875
- down_weight: bfloat16 [384, 512], replicated, may hold values from -0.5 to 0.5
Outputs:
- velocity: float32 [3, 8192, 128], P(None, ('leaf', 'rep'))
Inputs may be any that keep to these rules, and one draw needn't show every extreme that they name: `near_offset`: leaf g's near source leaves are (g + offset) mod 8192; slots at or past near_count are unused.
All inputs are finite; a program needn't handle non-finite values.
Results may differ from a plain program's by a relative error of at most 0.02.
Values may be sent and summed in bfloat16 or wider, within the bound.
A program may use at most 64 MiB of HBM per device.

v0:
```python
import math
import jax
import jax.numpy as jnp
from jax import lax
from jax.sharding import PartitionSpec as P


def padded(shard, sides, width):
    for axis, dim in sides:
        size, length = (lax.axis_size(axis), shard.shape[dim])
        up = [(i, (i + 1) % size) for i in range(size)]
        down = [(j, i) for i, j in up]
        last = lax.slice_in_dim(shard, length - width, length, axis=dim)
        first = lax.slice_in_dim(shard, 0, width, axis=dim)
        before = lax.ppermute(last, axis, up)
        after = lax.ppermute(first, axis, down)
        shard = jnp.concatenate([before, shard, after], axis=dim)
    return shard


def stokes_tile(target, source_pos, source_force, live_slots):
    offsets_xyz = target[:, None, :, None] - source_pos[:, :, None, :]
    distance_sq = jnp.sum(offsets_xyz * offsets_xyz, axis=0) + 0.05
    inverse = lax.rsqrt(distance_sq)
    inverse_cube = inverse * inverse * inverse
    projected = jnp.sum(offsets_xyz * source_force[:, :, None, :], axis=0)
    kernel_terms = source_force[:, :, None, :] * inverse + offsets_xyz * (projected * inverse_cube)
    kernel_terms = kernel_terms * live_slots[None, :, None, None]
    return jnp.sum(kernel_terms, axis=(1, 3)) * (1.0 / (8.0 * math.pi))


def body(
    positions,
    density,
    near_offset,
    near_count,
    inter_list,
    operator_index,
    lattice_index,
    up_weight,
    m2l_operators,
    lattice_operators,
    down_weight,
):
    per_box = positions.shape[1]
    node_count = positions.shape[2]
    kind_count = m2l_operators.shape[0]
    stacked = jnp.concatenate([positions, density], axis=0)
    extended = padded(stacked.astype(jnp.bfloat16), ((("leaf", "rep"), 1),), per_box).astype(
        stacked.dtype
    )
    slot_range = jnp.arange(near_offset.shape[1], dtype=jnp.int32)

    def one_leaf(leaf_slot):
        target = positions[:, leaf_slot]
        source_slot = leaf_slot + near_offset[leaf_slot] + per_box
        sources = jnp.take(extended, source_slot, axis=1)
        live_slots = (slot_range < near_count[leaf_slot]).astype(jnp.float32)
        return stokes_tile(target, sources[:3], sources[3:], live_slots)

    near_part = lax.map(one_leaf, jnp.arange(per_box, dtype=jnp.int32))
    near_part = jnp.transpose(near_part, (1, 0, 2))
    damping = 1.0 / (1.0 + jnp.sum(positions * positions, axis=0))
    summed = jnp.sum(density * damping[None], axis=1).reshape(-1).astype(jnp.bfloat16)
    coarse = jnp.dot(up_weight, summed, preferred_element_type=jnp.float32).astype(jnp.bfloat16)
    coarse_row = coarse.reshape(1, -1)
    box_ids = inter_list[0]
    op_kinds = operator_index[0]
    kind_range = jnp.arange(kind_count, dtype=jnp.int32)
    selector = (op_kinds[None, :] == kind_range[:, None]).astype(jnp.float32)
    all_blocks = lax.all_gather(coarse_row, ("leaf", "rep"), axis=0, tiled=True)
    chosen = jnp.take(all_blocks, box_ids, axis=0).astype(jnp.float32)
    grouped_sum = jnp.dot(selector, chosen, precision=lax.Precision.HIGHEST)
    block_sum = jnp.sum(all_blocks.astype(jnp.float32), axis=0)
    block_sum = lax.psum(coarse.astype(jnp.float32), ("leaf", "rep"))
    total = block_sum.astype(jnp.bfloat16)
    grouped = grouped_sum.astype(jnp.bfloat16)
    local = jnp.einsum("tij,tj->i", m2l_operators, grouped, preferred_element_type=jnp.float32)
    local = local + jnp.dot(
        lattice_operators[lattice_index[0]], total, preferred_element_type=jnp.float32
    )
    local_bf = local.astype(jnp.bfloat16)
    far_part = jnp.dot(down_weight, local_bf, preferred_element_type=jnp.float32).reshape(
        3, node_count
    )
    return near_part + damping[None] * far_part[:, None, :]


def solution(mesh):
    in_specs = (
        P(None, ("leaf", "rep"), None),
        P(None, ("leaf", "rep"), None),
        P(("leaf", "rep"), None),
        P(("leaf", "rep")),
        P(("leaf", "rep"), None),
        P(("leaf", "rep"), None),
        P(("leaf", "rep")),
        P(),
        P(),
        P(),
        P(),
    )
    out_specs = P(None, ("leaf", "rep"), None)
    return jax.shard_map(body, mesh=mesh, in_specs=in_specs, out_specs=out_specs, check_vma=False)
```

profile of v0, /device:TPU:4, one launch (start us, length us, event | category | flops | bytes accessed | tf_op | source)
XLA Modules:
  0.0 417.0 jit_solution(9846070013614672958)
XLA Ops:
  0.0 0.9 multiply_reduce_fusion.1
  0.9 0.8 multiply_reduce_fusion
  1.8 3.1 collective-permute-start
  4.9 2.7 collective-permute-start.1
  7.7 1.2 fusion.22
  8.9 108.3 %psum.7 = bf16[512]{0:T(512)(128)(2,1)S(1)} all-reduce(bf16[512]{0:T(512)(128)(2,1)S(1)} %convert_element_type.40), channel_id=1, replica_groups=mesh['leaf'=128,'rep'=4] {'leaf','rep'}, use_global_device_ids=true, to_apply=%region_7.8 | all-reduce | flops 512 | bytes 2048 | tf_op jit(solution)/shard_map/psum | solution.py:75
  117.8 136.1 %all-gather.1 = bf16[512,1,512]{2,1,0:T(2,128)(2,1)S(1)} all-gather(bf16[1,1,512]{2,1,0:T(2,128)(2,1)S(1)} %reshape.142), channel_id=2, replica_groups=mesh['leaf'=128,'rep'=4] {'leaf','rep'}, dimensions={0}, use_global_device_ids=true | all-gather | bytes 525312 | tf_op jit(solution)/shard_map/all_gather | solution.py:71
  254.2 1.0 gather_fusion.1
  256.0 1.3 fusion.10
  257.8 158.6 %while.13 = (s32[]{:T(128)}, f32[16,3,128]{2,0,1:T(8,128)S(1)}, s32[16]{0:T(128)S(1)}, s32[16,12]{1,0:T(8,128)}, f32[6,48,128]{2,0,1:T(8,128)S(1)}, /*index=5*/f...) while((s32[]{:T(128)}, f32[16,3,128]{2,0,1:T(8,128)S(1)}, ...), condition=%wide.region_4.5_spmd.clone, body=%wide.region_0.4_spmd.clone.sunk | while | flops 6891705 | bytes 6684707 | solution.py:61
  260.5 1.4 fusion.33
  262.5 1.4 compare_and_fusion.3
  264.0 0.7 constant_dynamic-slice_fusion.2
  270.4 1.4 fusion.33
  272.4 1.4 compare_and_fusion.3
  273.9 0.7 constant_dynamic-slice_fusion.2
  280.3 1.4 fusion.33
  282.3 1.4 compare_and_fusion.3
  290.3 1.4 fusion.33
  292.2 1.4 compare_and_fusion.3
  293.7 0.7 constant_dynamic-slice_fusion.2
  300.2 1.4 fusion.33
  302.1 1.4 compare_and_fusion.3
  310.1 1.4 fusion.33
  312.0 1.4 compare_and_fusion.3
  313.6 0.7 constant_dynamic-slice_fusion.2
  320.0 1.4 fusion.33
  322.0 1.4 compare_and_fusion.3
  323.5 0.7 constant_dynamic-slice_fusion.2
  329.9 1.4 fusion.33
  331.9 1.4 compare_and_fusion.3
  333.4 0.7 constant_dynamic-slice_fusion.2
  339.8 1.4 fusion.33
  341.8 1.4 compare_and_fusion.3
  349.7 1.4 fusion.33
  351.7 1.4 compare_and_fusion.3
  359.6 1.4 fusion.33
  361.6 1.4 compare_and_fusion.3
  369.6 1.4 fusion.33
  371.5 1.4 compare_and_fusion.3
  379.5 1.4 fusion.33
  381.4 1.4 compare_and_fusion.3
  389.4 1.4 fusion.33
  391.3 1.4 compare_and_fusion.3
  399.3 1.4 fusion.33
  401.3 1.4 compare_and_fusion.3
  409.2 1.4 fusion.33
  411.2 1.4 compare_and_fusion.3
  (298 shorter events, 77.1 us)
Async XLA Ops:
  0.0 255.4 %copy-start = (bf16[4,512,512]{2,1,0:T(8,128)(2,1)S(1)}, bf16[4,512,512]{2,1,0:T(8,128)(2,1)}, u32[]{:S(2)}) copy-start(bf16[4,512,512]{2,1,0:T(8,128)(2,1)} %param.21) | copy-start | bytes 6291460
  0.0 254.1 %copy-start.2 = (s32[1,189]{1,0:T(1,128)S(1)}, s32[1,189]{1,0:T(1,128)}, u32[]{:S(2)}) copy-start(s32[1,189]{1,0:T(1,128)} %param.17) | copy-start | bytes 2272
  1.8 255.9 %collective-permute-start = (bf16[6,16,128]{2,1,0:T(8,128)(2,1)S(1)}, bf16[6,16,128]{2,1,0:T(8,128)(2,1)S(1)}, u32[]{:S(2)}, u32[]{:S(2)}) collective-permute-start(bf16[6,16,128]{2,1,0:T(8,128)(2,1)S(1)} %pad_maximum_fusion), channel_id=1, source_target_pairs={{0,1},{1,2},{2,3},{3,4},{4,5},{5,6},{6,7},{7,8},{8,9},{9,10},{10,1... | collective-permute-start | bytes 73736 | tf_op jit(solution)/shard_map/ppermute | solution.py:15
  4.9 252.8 %collective-permute-start.1 = (bf16[6,16,128]{2,1,0:T(8,128)(2,1)S(1)}, bf16[6,16,128]{2,1,0:T(8,128)(2,1)S(1)}, u32[]{:S(2)}, u32[]{:S(2)}) collective-permute-start(bf16[6,16,128]{2,1,0:T(8,128)(2,1)S(1)} %pad_maximum_fusion), channel_id=1, source_target_pairs={{1,0},{2,1},{3,2},{4,3},{5,4},{6,5},{7,6},{8,7},{9,8},{10,9},{11,1... | collective-permute-start | bytes 73736 | tf_op jit(solution)/shard_map/ppermute | solution.py:16
  117.8 137.4 %copy-start.3 = (s32[1,189]{1,0:T(1,128)S(1)}, s32[1,189]{1,0:T(1,128)}, u32[]{:S(2)}) copy-start(s32[1,189]{1,0:T(1,128)} %param.18) | copy-start | bytes 2272
  254.1 3.2 copy-start.1
  255.2 2.6 copy-start.4
where the time goes:
time: 420 us; the launch traced here: 417 us
  blocking collectives  244 us (58%)
  other arithmetic  83.3 us (20%)
  local copies, waits for them, and re-layouts  44.2 us (11%)
  loops' own time  34.7 us (8%)
  starting transfers between devices  5.84 us (1%)
    all_gather x1, blocking collectives, body(): all_blocks = lax.all_gather(coarse_row, ('leaf', 'rep'), axis=0, tiled=True)  136 us
    psum x1, blocking collectives, body(): block_sum = lax.psum(coarse.astype(jnp.float32), ('leaf', 'rep'))  108 us
    another operation x1, loops' own time, body(): near_part = lax.map(one_leaf, jnp.arange(per_box, dtype=jnp.int32))  34.7 us
    select_n x32, other arithmetic, one_leaf(): sources = jnp.take(extended, source_slot, axis=1)  23.5 us
    and x16, other arithmetic, one_leaf(): sources = jnp.take(extended, source_slot, axis=1)  22.2 us
    dynamic_slice x32, local copies, waits for them, and re-layouts, one_leaf(): target = positions[:, leaf_slot]  11.6 us
    convert_element_type x16, other arithmetic, one_leaf(): live_slots = (slot_range < near_count[leaf_slot]).astype(jnp.float32)  11 us
    reduce_sum x16, other arithmetic, stokes_tile(): return jnp.sum(kernel_terms, axis=(1, 3)) * (1.0 / (8.0 * math.pi))  10.7 us
  transfers between devices with their start and end apart: 2, of which 0 were waited for; matrix products, arithmetic and copies ran while one was open for 1% of the time, Pallas kernels for 0%

commit v1 on v0

--- a/solution.py
+++ b/solution.py
@@ -68,7 +68,12 @@
     op_kinds = operator_index[0]
     kind_range = jnp.arange(kind_count, dtype=jnp.int32)
     selector = (op_kinds[None, :] == kind_range[:, None]).astype(jnp.float32)
-    all_blocks = lax.all_gather(coarse_row, ("leaf", "rep"), axis=0, tiled=True)
+    all_blocks = jnp.concatenate(
+        lax.all_to_all(
+            jnp.stack([coarse_row] * lax.axis_size(("leaf", "rep"))), ("leaf", "rep"), 0, 0
+        ),
+        axis=0,
+    )
     chosen = jnp.take(all_blocks, box_ids, axis=0).astype(jnp.float32)
     grouped_sum = jnp.dot(selector, chosen, precision=lax.Precision.HIGHEST)
     block_sum = jnp.sum(all_blocks.astype(jnp.float32), axis=0)

time: 420 us -> 320 us (0.76)
  the two profiles are of different devices: /device:TPU:4 before, /device:TPU:1 now
where the time goes in v1:
time: 320 us; the launch traced here: 317 us
  blocking collectives  109 us (34%)
  other arithmetic  88.2 us (28%)
  local copies, waits for them, and re-layouts  50.3 us (16%)
  loops' own time  34.8 us (11%)
  starting transfers between devices  30.2 us (9%)
  matrix products  3.58 us (1%)
    psum x1, blocking collectives, body(): block_sum = lax.psum(coarse.astype(jnp.float32), ('leaf', 'rep'))  109 us
    another operation x1, loops' own time, body(): near_part = lax.map(one_leaf, jnp.arange(per_box, dtype=jnp.int32))  34.8 us
    select_n x32, other arithmetic, one_leaf(): sources = jnp.take(extended, source_slot, axis=1)  23.5 us
    all_to_all x1, starting transfers between devices, body(): lax.all_to_all(jnp.stack([coarse_row] * lax.axis_size(('leaf', 'rep'))),...  22.5 us
    and x16, other arithmetic, one_leaf(): sources = jnp.take(extended, source_slot, axis=1)  22.3 us
    dynamic_slice x32, local copies, waits for them, and re-layouts, one_leaf(): target = positions[:, leaf_slot]  11.6 us
    convert_element_type x16, other arithmetic, one_leaf(): live_slots = (slot_range < near_count[leaf_slot]).astype(jnp.float32)  11.1 us
    reduce_sum x16, other arithmetic, stokes_tile(): return jnp.sum(kernel_terms, axis=(1, 3)) * (1.0 / (8.0 * math.pi))  11 us
  transfers between devices with their start and end apart: 3, of which 0 were waited for; matrix products, arithmetic and copies ran while one was open for 42% of the time, Pallas kernels for 0%

profile of v1, /device:TPU:1, one launch (start us, length us, event | category | flops | bytes accessed | tf_op | source)
XLA Modules:
  0.0 316.6 jit_solution(16698145227748254225)
XLA Ops:
  0.0 0.9 multiply_reduce_fusion.1
  0.9 0.8 multiply_reduce_fusion
  1.8 3.9 %collective-permute-start = (bf16[6,16,128]{2,1,0:T(8,128)(2,1)S(1)}, bf16[6,16,128]{2,1,0:T(8,128)(2,1)S(1)}, u32[]{:S(2)}, u32[]{:S(2)}) collective-permute-start(bf16[6,16,128]{2,1,0:T(8,128)(2,1)S(1)} %pad_maximum_fusion), channel_id=1, source_target_pairs={{0,1},{1,2},{2,3},{3,4},{4,5},{5,6},{6,7},{7,8},{8,9},{9,10},{10,1... | collective-permute-start | bytes 73736 | tf_op jit(solution)/shard_map/ppermute | solution.py:15
  5.7 3.7 %collective-permute-start.1 = (bf16[6,16,128]{2,1,0:T(8,128)(2,1)S(1)}, bf16[6,16,128]{2,1,0:T(8,128)(2,1)S(1)}, u32[]{:S(2)}, u32[]{:S(2)}) collective-permute-start(bf16[6,16,128]{2,1,0:T(8,128)(2,1)S(1)} %pad_maximum_fusion), channel_id=1, source_target_pairs={{1,0},{2,1},{3,2},{4,3},{5,4},{6,5},{7,6},{8,7},{9,8},{10,9},{11,1... | collective-permute-start | bytes 73736 | tf_op jit(solution)/shard_map/ppermute | solution.py:16
  9.5 1.2 fusion.22
  11.8 4.6 %reduce.2 = bf16[512,512]{1,0:T(8,128)(2,1)} reduce(bf16[512,1,512]{2,1,0:T(2,128)(2,1)S(1)} %stack.3, bf16[]{:T(256)} %broadcast.198), dimensions={1}, to_apply=%stack.3.reduce_sub_computation | reduce | bytes 1048578 | tf_op jit(solution)/shard_map/stack | solution.py:73
  16.4 2.0 reshape.156
  18.4 22.5 %all-to-all-start = ((bf16[512,2,256]{2,1,0:T(2,128)(2,1)}), bf16[512,2,256]{2,1,0:T(2,128)(2,1)S(1)}, u32[]{:S(2)}, u32[]{:S(2)}) async-start(bf16[512,2,256]{2,1,0:T(2,128)(2,1)} %reshape.156), calls=%async_computation | async-start | bytes 1048576 | tf_op jit(solution)/shard_map/all_to_all | solution.py:72
  40.9 108.7 %psum.7 = bf16[512]{0:T(512)(128)(2,1)S(1)} all-reduce(bf16[512]{0:T(512)(128)(2,1)S(1)} %convert_element_type.40), channel_id=1, replica_groups=mesh['leaf'=128,'rep'=4] {'leaf','rep'}, use_global_device_ids=true, to_apply=%region_7.8 | all-reduce | flops 512 | bytes 2048 | tf_op jit(solution)/shard_map/psum | solution.py:80
  150.3 1.3 fusion.10
  151.7 159.0 %while.13 = (s32[]{:T(128)}, f32[16,3,128]{2,0,1:T(8,128)S(1)}, s32[16]{0:T(128)S(1)}, s32[16,12]{1,0:T(8,128)}, f32[6,48,128]{2,0,1:T(8,128)S(1)}, /*index=5*/f...) while((s32[]{:T(128)}, f32[16,3,128]{2,0,1:T(8,128)S(1)}, ...), condition=%wide.region_4.5_spmd.clone, body=%wide.region_0.4_spmd.clone.sunk | while | flops 6891705 | bytes 6684707 | solution.py:61
  154.5 1.4 fusion.33
  156.4 1.4 compare_and_fusion.3
  158.0 0.7 constant_dynamic-slice_fusion.2
  164.4 1.4 fusion.33
  166.4 1.4 compare_and_fusion.3
  167.9 0.7 constant_dynamic-slice_fusion.2
  174.4 1.4 fusion.33
  176.3 1.4 compare_and_fusion.3
  184.3 1.4 fusion.33
  186.3 1.4 compare_and_fusion.3
  194.2 1.4 fusion.33
  196.2 1.4 compare_and_fusion.3
  204.2 1.4 fusion.33
  206.1 1.4 compare_and_fusion.3
  214.1 1.4 fusion.33
  216.1 1.4 compare_and_fusion.3
  224.0 1.4 fusion.33
  226.0 1.4 compare_and_fusion.3
  234.0 1.4 fusion.33
  235.9 1.4 compare_and_fusion.3
  243.9 1.4 fusion.33
  245.9 1.4 compare_and_fusion.3
  253.8 1.4 fusion.33
  255.8 1.4 compare_and_fusion.3
  263.8 1.4 fusion.33
  265.7 1.4 compare_and_fusion.3
  273.7 1.4 fusion.33
  275.7 1.4 compare_and_fusion.3
  283.7 1.4 fusion.33
  285.6 1.4 compare_and_fusion.3
  293.6 1.4 fusion.33
  295.6 1.4 compare_and_fusion.3
  303.5 1.4 fusion.33
  305.5 1.4 compare_and_fusion.3
  310.7 1.7 reshape.157
  312.5 1.3 copy.51
  313.8 1.0 gather_fusion.1
  (303 shorter events, 81.3 us)
Async XLA Ops:
  0.0 315.1 %copy-start = (bf16[4,512,512]{2,1,0:T(8,128)(2,1)S(1)}, bf16[4,512,512]{2,1,0:T(8,128)(2,1)}, u32[]{:S(2)}) copy-start(bf16[4,512,512]{2,1,0:T(8,128)(2,1)} %param.21) | copy-start | bytes 6291460
  1.8 149.8 %collective-permute-start = (bf16[6,16,128]{2,1,0:T(8,128)(2,1)S(1)}, bf16[6,16,128]{2,1,0:T(8,128)(2,1)S(1)}, u32[]{:S(2)}, u32[]{:S(2)}) collective-permute-start(bf16[6,16,128]{2,1,0:T(8,128)(2,1)S(1)} %pad_maximum_fusion), channel_id=1, source_target_pairs={{0,1},{1,2},{2,3},{3,4},{4,5},{5,6},{6,7},{7,8},{8,9},{9,10},{10,1... | collective-permute-start | bytes 73736 | tf_op jit(solution)/shard_map/ppermute | solution.py:15
  5.7 145.9 %collective-permute-start.1 = (bf16[6,16,128]{2,1,0:T(8,128)(2,1)S(1)}, bf16[6,16,128]{2,1,0:T(8,128)(2,1)S(1)}, u32[]{:S(2)}, u32[]{:S(2)}) collective-permute-start(bf16[6,16,128]{2,1,0:T(8,128)(2,1)S(1)} %pad_maximum_fusion), channel_id=1, source_target_pairs={{1,0},{2,1},{3,2},{4,3},{5,4},{6,5},{7,6},{8,7},{9,8},{10,9},{11,1... | collective-permute-start | bytes 73736 | tf_op jit(solution)/shard_map/ppermute | solution.py:16
  11.3 139.0 %copy-start.2 = (s32[1,189]{1,0:T(1,128)S(1)}, s32[1,189]{1,0:T(1,128)}, u32[]{:S(2)}) copy-start(s32[1,189]{1,0:T(1,128)} %param.17) | copy-start | bytes 2272
  11.8 139.9 %copy-start.4 = (s32[16]{0:T(128)S(1)}, s32[16]{0:T(128)}, u32[]{:S(2)}) copy-start(s32[16]{0:T(128)} %param.16) | copy-start | bytes 196
  18.4 292.3 %all-to-all-start = ((bf16[512,2,256]{2,1,0:T(2,128)(2,1)}), bf16[512,2,256]{2,1,0:T(2,128)(2,1)S(1)}, u32[]{:S(2)}, u32[]{:S(2)}) async-start(bf16[512,2,256]{2,1,0:T(2,128)(2,1)} %reshape.156), calls=%async_computation | async-start | bytes 1048576 | tf_op jit(solution)/shard_map/all_to_all | solution.py:72
  310.7 4.1 %copy-start.3 = (s32[1,189]{1,0:T(1,128)S(1)}, s32[1,189]{1,0:T(1,128)}, u32[]{:S(2)}) copy-start(s32[1,189]{1,0:T(1,128)} %param.18) | copy-start | bytes 2272
  313.8 1.9 copy-start.1
